TPU v7x, 32 devices: a whole 2x2x4 slice. The times are simulated.
32 devices in a mesh: ctx: 4 (over y, x), fsdp: 8 (over z, core).
Axes of the slice: x: 2, y: 2, z: 4, core: 2. Of those that a mesh axis runs over, the one named last changes fastest.
Arguments:
- tokens: bfloat16 [8, 2560, 2048], P('fsdp', 'ctx'), may hold values from -6 to 6
- cotangent: bfloat16 [8, 2560, 2048], P('fsdp', 'ctx'), may hold values from -6 to 6
- block_table: int32 [8, 40], P('fsdp'), may hold values from 0 to 39, as said below
- ln_gain: bfloat16 [2048], replicated, may hold values from 0.5 to 1.5
- ln_bias: bfloat16 [2048], replicated, may hold values from -2 to 2
- w_qkv: bfloat16 [2048, 3, 2048], P('fsdp', None, 'ctx'), may hold values from -0.125 to 0.125
- b_qkv: bfloat16 [6144], replicated, may hold values from -2 to 2
- w_dense: bfloat16 [2048, 2048], P('ctx', 'fsdp'), may hold values from -0.5 to 0.5
- b_dense: bfloat16 [2048], replicated, may hold values from -2 to 2
- w_fc1: bfloat16 [2048, 8192], P('fsdp', 'ctx'), may hold values from -0.125 to 0.125
- b_fc1: bfloat16 [8192], replicated, may hold values from -2 to 2
- w_fc2: bfloat16 [8192, 2048], P('ctx', 'fsdp'), may hold values from -0.0625 to 0.0625
- b_fc2: bfloat16 [2048], replicated, may hold values from -2 to 2
Outputs:
- output: bfloat16 [8, 2560, 2048], P('fsdp', 'ctx')
- d_tokens: bfloat16 [8, 2560, 2048], P('fsdp', 'ctx')
- d_ln_gain: float32 [2048], replicated
- d_ln_bias: float32 [2048], replicated
- d_w_qkv: float32 [2048, 3, 2048], P('fsdp', None, 'ctx')
- d_b_qkv: float32 [6144], replicated
- d_w_dense: float32 [2048, 2048], P('ctx', 'fsdp')
- d_b_dense: float32 [2048], replicated
- d_w_fc1: float32 [2048, 8192], P('fsdp', 'ctx')
- d_b_fc1: float32 [8192], replicated
- d_w_fc2: float32 [8192, 2048], P('ctx', 'fsdp')
- d_b_fc2: float32 [2048], replicated
Inputs may be any that keep to these rules, and one draw needn't show every extreme that they name: `block_table`: each row lists each of the 40 blocks of its group exactly once.
All inputs are finite; a program needn't handle non-finite values.
Results may differ from a plain program's by a relative error of at most 0.015.
Values may be sent and summed in bfloat16 or wider, within the bound.
No kernel may reach another device: no remote copies, remote signals or barrier semaphores. Data moves between devices by JAX's collectives and lax.ppermute only.
A program may use at most 832 MiB of HBM per device.

v0:
```python
import math
import jax
import jax.numpy as jnp
from jax import lax
from jax.sharding import PartitionSpec as P

HEADS = 32
ROT = 32
PROMPT = 2048
CLEN = 256
BLK = 64


def layer_norm(values, gain, shift):
    average = jnp.mean(values, axis=-1, keepdims=True)
    centred = values - average
    variance = jnp.mean(centred * centred, axis=-1, keepdims=True)
    return centred * lax.rsqrt(variance + 1e-05) * gain + shift


def gelu_tanh(values):
    return (
        0.5
        * values
        * (
            1.0
            + jnp.tanh(math.sqrt(2.0 / math.pi) * (values + 0.044715 * values * values * values))
        )
    )


def segment_of(places):
    return jnp.where(places < PROMPT, 0, 1 + (places - PROMPT) // CLEN)


def position_of(places):
    return jnp.where(places < PROMPT, places, PROMPT + (places - PROMPT) % CLEN)


def visible(query_places, key_places):
    query_segment = segment_of(query_places)
    key_segment = segment_of(key_places)
    return (key_segment == 0) & (query_segment > 0) | (key_segment == query_segment) & (
        key_places <= query_places
    )


def frequencies():
    half_dims = ROT // 2
    return 10000.0 ** (-2.0 * jnp.arange(half_dims, dtype=jnp.float32) / ROT)


def rotate(values, angles, head_dim):
    row_count = values.shape[0]
    by_head = values.reshape(row_count, -1, head_dim)
    half_dims = angles.shape[1]
    cosine = jnp.cos(angles)[:, None, :]
    sine_part = jnp.sin(angles)[:, None, :]
    front = by_head[:, :, :half_dims]
    second = by_head[:, :, half_dims : 2 * half_dims]
    turned = jnp.concatenate(
        [
            front * cosine - second * sine_part,
            second * cosine + front * sine_part,
            by_head[:, :, 2 * half_dims :],
        ],
        axis=-1,
    )
    return turned.reshape(row_count, -1)


def product(left, right):
    return jnp.dot(left, right, preferred_element_type=jnp.float32)


def contract_rows(left, right):
    return lax.dot_general(
        left, right, (((0,), (0,)), ((), ())), preferred_element_type=jnp.float32
    )


def contract_cols(left, right):
    return lax.dot_general(
        left, right, (((1,), (1,)), ((), ())), preferred_element_type=jnp.float32
    )


def shards(
    tokens,
    cotangent,
    block_table,
    ln_gain,
    ln_bias,
    w_qkv,
    b_qkv,
    w_dense,
    b_dense,
    w_fc1,
    b_fc1,
    w_fc2,
    b_fc2,
):
    group_count, local_rows, width = tokens.shape
    head_dim = width // HEADS
    scale = 1.0 / math.sqrt(head_dim)
    ctx_count = lax.axis_size("ctx")
    ctx_index = lax.axis_index("ctx")
    group_rows = local_rows * ctx_count
    hidden_whole = b_fc1.shape[0]
    dense_each = width // ctx_count
    hidden_each = hidden_whole // ctx_count
    local_blocks = local_rows // BLK
    own_blocks = lax.dynamic_slice_in_dim(block_table, ctx_index * local_blocks, local_blocks, 1)
    offsets = jnp.arange(BLK, dtype=jnp.int32)
    own_place = (own_blocks[:, :, None] * BLK + offsets[None, None, :]).reshape(
        group_count, local_rows
    )
    key_place = (block_table[:, :, None] * BLK + offsets[None, None, :]).reshape(
        group_count, group_rows
    )
    flat_tokens = tokens.reshape(group_count * local_rows, width).astype(jnp.float32)
    grad_values = cotangent.reshape(group_count * local_rows, width).astype(jnp.float32)
    normed, norm_pull = jax.vjp(
        layer_norm, flat_tokens, ln_gain.astype(jnp.float32), ln_bias.astype(jnp.float32)
    )
    normed_low = normed.astype(jnp.bfloat16)
    qkv_weight, fc1_weight, dense_weight, fc2_weight = (
        lax.all_gather(w_qkv, "ctx", axis=2, tiled=True),
        lax.all_gather(w_fc1, "ctx", axis=1, tiled=True),
        lax.all_gather(w_dense, "ctx", axis=0, tiled=True),
        lax.all_gather(w_fc2, "ctx", axis=0, tiled=True),
    )
    grad_rows = cotangent.reshape(-1, width)
    row_count = normed_low.shape[0]
    query_rows = row_count // group_count
    qkv_cols = qkv_weight.shape[2]
    head_total = qkv_cols // head_dim
    pieces = (
        lax.all_gather(qkv_weight, "fsdp", axis=0, tiled=True),
        lax.all_gather(fc1_weight, "fsdp", axis=0, tiled=True),
    )
    piece_rows = pieces[0].shape[0]
    columns = normed_low
    projected = product(columns, pieces[0].reshape(piece_rows, -1))
    expanded = product(columns, pieces[1])
    qkv_bias = b_qkv.reshape(3, width).reshape(-1)
    projected = projected + qkv_bias.astype(jnp.float32)
    expanded = expanded + b_fc1.astype(jnp.float32)
    angles = (
        position_of(own_place.reshape(row_count)).astype(jnp.float32)[:, None]
        * frequencies()[None, :]
    )

    def turn(pair_values):
        return rotate(pair_values, angles, head_dim)

    turned, turn_pull = jax.vjp(turn, projected[:, : 2 * qkv_cols])
    query_low = turned[:, :qkv_cols].astype(jnp.bfloat16).reshape(group_count, query_rows, qkv_cols)
    key_low = turned[:, qkv_cols:].astype(jnp.bfloat16).reshape(group_count, query_rows, qkv_cols)
    value_low = (
        projected[:, 2 * qkv_cols :].astype(jnp.bfloat16).reshape(group_count, query_rows, qkv_cols)
    )
    key_all, value_all = (
        lax.all_gather(key_low, "ctx", axis=1, tiled=True),
        lax.all_gather(value_low, "ctx", axis=1, tiled=True),
    )
    heads_each = min(8, head_total)
    block_count = query_rows // query_rows

    def split_heads(values):
        shaped = values.reshape(
            values.shape[0], values.shape[1], head_total // heads_each, heads_each, head_dim
        )
        return jnp.moveaxis(shaped, 2, 0)

    def join_heads(values):
        moved = jnp.moveaxis(values, 0, 2)
        return moved.reshape(moved.shape[0], moved.shape[1], qkv_cols)

    def split_rows(values):
        shaped = values.reshape((values.shape[0], block_count, query_rows) + values.shape[2:])
        return jnp.moveaxis(shaped, 1, 0)

    def join_rows(values):
        moved = jnp.moveaxis(values, 0, 1)
        return moved.reshape((moved.shape[0], query_rows) + moved.shape[3:])

    place_blocks = split_rows(own_place)

    def scores_of(query_part, key_part, place_part):
        allowed = visible(place_part[:, :, None], key_place[:, None, :])
        raw = (
            jnp.einsum("gqhe,gkhe->ghqk", query_part, key_part, preferred_element_type=jnp.float32)
            * scale
        )
        return (jnp.where(allowed[:, None], raw, -1e30), allowed)

    def forward_heads(operands):
        query_part, key_part, value_part = operands

        def forward_one_block(items):
            query_block, place_block = items
            scores, allowed = scores_of(query_block, key_part, place_block)
            top_score = jnp.max(scores, axis=-1, keepdims=True)
            summed_exp = jnp.sum(jnp.exp(scores - top_score), axis=-1, keepdims=True)
            log_total = top_score + jnp.log(summed_exp)
            weights = jnp.where(allowed[:, None], jnp.exp(scores - log_total), 0.0)
            mixed = jnp.einsum(
                "ghqk,gkhe->gqhe",
                weights.astype(jnp.bfloat16),
                value_part,
                preferred_element_type=jnp.float32,
            )
            return (mixed, log_total)

        mixed, log_total = lax.map(forward_one_block, (split_rows(query_part), place_blocks))
        return (join_rows(mixed), log_total)

    attended, log_totals = lax.map(
        forward_heads, (split_heads(query_low), split_heads(key_all), split_heads(value_all))
    )
    attended_low = join_heads(attended).reshape(row_count, qkv_cols).astype(jnp.bfloat16)
    activated, gelu_pull = jax.vjp(gelu_tanh, expanded)
    activated_low = activated.astype(jnp.bfloat16)
    pieces = (
        lax.all_gather(dense_weight, "fsdp", axis=1, tiled=True),
        lax.all_gather(fc2_weight, "fsdp", axis=1, tiled=True),
    )
    part_sum = product(attended_low, pieces[0]) + product(activated_low, pieces[1])
    summed = part_sum
    result = flat_tokens + summed + b_dense.astype(jnp.float32) + b_fc2.astype(jnp.float32)
    output = result.astype(jnp.bfloat16).reshape(group_count, local_rows, width)
    out_bias_grad = jnp.sum(grad_values, axis=0)
    out_each = dense_each + hidden_each

    def out_block(index):
        attended_part = lax.dynamic_slice_in_dim(attended_low, index * dense_each, dense_each, 1)
        activated_part = lax.dynamic_slice_in_dim(
            activated_low, index * hidden_each, hidden_each, 1
        )
        return jnp.concatenate(
            [contract_rows(attended_part, grad_rows), contract_rows(activated_part, grad_rows)],
            axis=0,
        )

    blocks = lax.map(
        out_block, jnp.arange(out_each * lax.axis_size("ctx") // out_each, dtype=jnp.int32)
    )
    out_local = lax.psum_scatter(
        blocks.reshape(out_each * lax.axis_size("ctx"), width).astype(jnp.bfloat16),
        "ctx",
        scatter_dimension=0,
        tiled=True,
    )
    pieces = (
        lax.all_gather(dense_weight, "fsdp", axis=1, tiled=True),
        lax.all_gather(fc2_weight, "fsdp", axis=1, tiled=True),
    )
    columns = grad_rows
    attended_grad = contract_cols(columns, pieces[0])
    activated_grad = contract_cols(columns, pieces[1])
    attended_grad_low = attended_grad.astype(jnp.bfloat16).reshape(
        group_count, query_rows, qkv_cols
    )
    expanded_grad = gelu_pull(activated_grad)[0].astype(jnp.bfloat16)

    def backward_heads(operands):
        query_part, key_part, value_part, grad_part, log_total = operands

        def backward_one_block(carry, items):
            query_block, grad_block, place_block, log_block = items
            scores, allowed = scores_of(query_block, key_part, place_block)
            weights = jnp.where(allowed[:, None], jnp.exp(scores - log_block), 0.0)
            weight_grad = jnp.einsum(
                "gqhe,gkhe->ghqk", grad_block, value_part, preferred_element_type=jnp.float32
            )
            inner = jnp.sum(weights * weight_grad, axis=-1, keepdims=True)
            score_grad = (weights * (weight_grad - inner)).astype(jnp.bfloat16)
            query_grad = (
                jnp.einsum(
                    "ghqk,gkhe->gqhe", score_grad, key_part, preferred_element_type=jnp.float32
                )
                * scale
            )
            key_grad = (
                carry[0]
                + jnp.einsum(
                    "ghqk,gqhe->gkhe", score_grad, query_block, preferred_element_type=jnp.float32
                )
                * scale
            )
            value_grad = carry[1] + jnp.einsum(
                "ghqk,gqhe->gkhe",
                weights.astype(jnp.bfloat16),
                grad_block,
                preferred_element_type=jnp.float32,
            )
            return ((key_grad, value_grad), query_grad)

        zero_grad = jnp.zeros(key_part.shape, jnp.float32)
        sums, query_grad = lax.scan(
            backward_one_block,
            (zero_grad, zero_grad),
            (split_rows(query_part), split_rows(grad_part), place_blocks, log_total),
        )
        return (join_rows(query_grad), sums[0], sums[1])

    query_grads, key_grads, value_grads = lax.map(
        backward_heads,
        (
            split_heads(query_low),
            split_heads(key_all),
            split_heads(value_all),
            split_heads(attended_grad_low),
            log_totals,
        ),
    )
    key_full = join_heads(key_grads)
    value_full = join_heads(value_grads)
    key_mine, value_mine = (
        lax.psum_scatter(
            key_full.astype(jnp.bfloat16), "ctx", scatter_dimension=1, tiled=True
        ).astype(jnp.float32),
        lax.psum_scatter(
            value_full.astype(jnp.bfloat16), "ctx", scatter_dimension=1, tiled=True
        ).astype(jnp.float32),
    )
    pair_grad = jnp.concatenate(
        [
            join_heads(query_grads).reshape(row_count, qkv_cols),
            key_mine.reshape(row_count, qkv_cols),
        ],
        axis=1,
    )
    turned_back = turn_pull(pair_grad)[0]
    projected_grad = jnp.concatenate(
        [turned_back, value_mine.reshape(row_count, qkv_cols)], axis=1
    ).astype(jnp.bfloat16)
    grad_by_part = projected_grad.reshape(row_count, 3, qkv_cols)

    def in_block(index):
        qkv_part = lax.dynamic_slice_in_dim(
            grad_by_part, index * dense_each, dense_each, 2
        ).reshape(row_count, 3 * dense_each)
        hidden_part = lax.dynamic_slice_in_dim(expanded_grad, index * hidden_each, hidden_each, 1)
        return jnp.concatenate(
            [contract_rows(normed_low, qkv_part), contract_rows(normed_low, hidden_part)], axis=1
        )

    span_rows = width * lax.axis_size("ctx")
    blocks = lax.map(in_block, jnp.arange(span_rows // width, dtype=jnp.int32))
    in_local = lax.psum_scatter(
        blocks.reshape(span_rows, -1).astype(jnp.bfloat16), "ctx", scatter_dimension=0, tiled=True
    )
    qkv_bias_part = jnp.sum(projected_grad.astype(jnp.float32), axis=0).reshape(3, qkv_cols)
    qkv_bias_grad = qkv_bias_part.reshape(-1)
    fc1_bias_part = jnp.sum(expanded_grad.astype(jnp.float32), axis=0)
    pieces = (
        lax.all_gather(qkv_weight, "fsdp", axis=0, tiled=True),
        lax.all_gather(fc1_weight, "fsdp", axis=0, tiled=True),
    )
    piece_rows = pieces[0].shape[0]
    part_sum = contract_cols(projected_grad, pieces[0].reshape(piece_rows, -1)) + contract_cols(
        expanded_grad, pieces[1]
    )
    out_share, in_share = (
        lax.psum_scatter(out_local, "fsdp", scatter_dimension=1, tiled=True).astype(jnp.float32),
        lax.psum_scatter(in_local, "fsdp", scatter_dimension=0, tiled=True).astype(jnp.float32),
    )
    d_w_dense = out_share[:dense_each]
    d_w_fc2 = out_share[dense_each:]
    d_w_qkv = in_share[:, : 3 * dense_each].reshape(-1, 3, dense_each)
    d_w_fc1 = in_share[:, 3 * dense_each :]
    token_grad_norm, gain_grad, shift_grad = norm_pull(part_sum)
    d_tokens = (
        (grad_values + token_grad_norm).astype(jnp.bfloat16).reshape(group_count, local_rows, width)
    )
    gain_sum, shift_sum, qkv_bias_sum, out_bias_sum, fc1_bias_sum = lax.psum(
        (gain_grad, shift_grad, qkv_bias_grad, out_bias_grad, fc1_bias_part), ("ctx", "fsdp")
    )
    return (
        output,
        d_tokens,
        gain_sum,
        shift_sum,
        d_w_qkv,
        qkv_bias_sum,
        d_w_dense,
        out_bias_sum,
        d_w_fc1,
        fc1_bias_sum,
        d_w_fc2,
        out_bias_sum,
    )


def solution(mesh):
    in_specs = (
        P("fsdp", "ctx", None),
        P("fsdp", "ctx", None),
        P("fsdp", None),
        P(),
        P(),
        P("fsdp", None, "ctx"),
        P(),
        P("ctx", "fsdp"),
        P(),
        P("fsdp", "ctx"),
        P(),
        P("ctx", "fsdp"),
        P(),
    )
    out_specs = (
        P("fsdp", "ctx", None),
        P("fsdp", "ctx", None),
        P(),
        P(),
        P("fsdp", None, "ctx"),
        P(),
        P("ctx", "fsdp"),
        P(),
        P("fsdp", "ctx"),
        P(),
        P("ctx", "fsdp"),
        P(),
    )
    return jax.shard_map(shards, mesh=mesh, in_specs=in_specs, out_specs=out_specs, check_vma=False)
```

profile of v0, /device:TPU:0, one launch (start us, length us, event | category | flops | bytes accessed | tf_op | source)
XLA Modules:
  0.0 3172.5 jit_solution(17487051022101723926)
XLA Ops:
  10.5 46.7 %all-gather.13.cloned.1.call-done = bf16[256,3,2048]{0,2,1:T(8,128)(2,1)} async-done(((bf16[256,3,512]{0,2,1:T(8,128)(2,1)}), bf16[256,3,2048]{0,2,1:T(8,128)(2,1)}) %all-gather.13.cloned.1.call-update) | async-done | bytes 3145744 | tf_op jit(solution)/shard_map/all_gather | solution.py:128
  58.4 27.3 all-gather.17.cloned.1.call-done
  87.7 220.7 %all-gather.15.cloned.1.call-done = bf16[2048,3,2048]{0,2,1:T(8,128)(2,1)} async-done(((bf16[256,3,2048]{0,2,1:T(8,128)(2,1)}), bf16[2048,3,2048]{0,2,1:T(8,128)(2,1)}) %all-gather.15.cloned.1.call-update) | async-done | bytes 25165840 | tf_op jit(solution)/shard_map/all_gather | solution.py:139
  308.5 22.6 convolution_add_fusion
  369.6 46.2 %all-gather.25.cloned.1.call-done = bf16[8192,256]{1,0:T(8,128)(2,1)} async-done(((bf16[2048,256]{1,0:T(8,128)(2,1)}), bf16[8192,256]{1,0:T(8,128)(2,1)}) %all-gather.25.cloned.1.call-update) | async-done | bytes 4194320 | tf_op jit(solution)/shard_map/all_gather | solution.py:131
  416.3 83.4 %all-gather.19.cloned.1.call-done = bf16[2048,2048]{1,0:T(8,128)(2,1)} async-done(((bf16[2048,256]{1,0:T(8,128)(2,1)}), bf16[2048,2048]{1,0:T(8,128)(2,1)}) %all-gather.19.cloned.1.call-update) | async-done | bytes 8388624 | tf_op jit(solution)/shard_map/all_gather | solution.py:226
  512.0 93.4 %all-gather.29.cloned.1.call-done = bf16[2560,2048]{1,0:T(8,128)(2,1)} async-done(((bf16[640,2048]{1,0:T(8,128)(2,1)}), bf16[2560,2048]{1,0:T(8,128)(2,1)}) %all-gather.29.cloned.1.call-update) | async-done | bytes 10485776 | tf_op jit(solution)/shard_map/all_gather | solution.py:165
  619.7 92.8 %all-gather.31.cloned.1.call-done = bf16[2560,2048]{0,1:T(8,128)(2,1)} async-done(((bf16[640,2048]{0,1:T(8,128)(2,1)}), bf16[2560,2048]{0,1:T(8,128)(2,1)}) %all-gather.31.cloned.1.call-update) | async-done | bytes 10485776 | tf_op jit(solution)/shard_map/all_gather | solution.py:164
  712.4 278.3 %while.71 = (s32[]{:T(128)}, bf16[4,1,640,8,64]{2,4,3,1,0:T(8,128)(2,1)}, f32[4,1,1,8,640,1]{4,3,5,2,1,0:T(8,128)S(1)}, bf16[4,1,2560,8,64]{2,4,3,1,0:T(8,128)(2...) while((s32[]{:T(128)}, ...), condition=%wide.region_5.6_spmd.clone.clone, body=%wide.region_2.5_spmd.clone.sunk.clone | while | flops 3520983552 | bytes 171326496 | solution.py:219
  715.5 27.3 fusion.228
  742.8 20.4 exponential_reduce_fusion.3
  763.2 22.7 fusion.229
  788.9 22.4 fusion.228
  811.3 20.4 exponential_reduce_fusion.3
  831.7 22.6 fusion.229
  857.4 22.4 fusion.228
  879.8 20.4 exponential_reduce_fusion.3
  900.2 22.5 fusion.229
  925.8 22.1 fusion.228
  947.9 20.3 exponential_reduce_fusion.3
  968.2 22.5 fusion.229
  990.7 649.2 %while.72 = (s32[]{:T(128)}, f32[4,1,640,8,64]{2,4,3,1,0:T(8,128)}, bf16[4,1,2560,8,64]{2,4,3,1,0:T(8,128)(2,1)}, bf16[4,1,2560,8,64]{2,4,3,1,0:T(8,128)(2,1)}, ...) while((s32[]{:T(128)}, f32[4,1,640,8,64]{2,4,3,1,0:T(8,128)}, ...), condition=%wide.region_8.9_spmd.clone.clone, body=%wide.region_6.8_spmd.clone.sunk.clone | while | flops 8529572352 | bytes 418994240 | solution.py:308
  993.9 26.3 fusion.238
  1020.2 45.3 %multiply_reduce_fusion.3 = (f32[8,640]{1,0:T(8,128)S(1)}, f32[8,640,2560]{2,1,0:T(8,128)}) fusion(f32[8,640,2560]{2,1,0:T(8,128)} %fusion.238, f32[8,640]{1,0:T(8,128)S(1)} %dynamic-slice_bitcast_fusion.3, bf16[4,1,2560,8,64]{2,4,3,1,0:T(8,128)(2,1)} %get-tuple-element.1049, s32[]{:T(128)} %get-tuple-element.1034, ...), kind=kOutput, calls=%fused_computation.66.clone.1.clone | convolution fusion | flops 1756359680 | bytes 109814784 | tf_op jit(solution)/shard_map/while/body/eval_jaxpr/while/body/eval_jaxpr/gqhe,gkhe->ghqk/dot_general | solution.py:193
  1065.6 42.1 %multiply_convert_fusion.4 = bf16[8,640,2560]{2,1,0:T(8,128)(2,1)} fusion(f32[8,640,2560]{2,1,0:T(8,128)} %get-tuple-element.985, f32[8,640,2560]{2,1,0:T(8,128)} %fusion.238, f32[8,640]{1,0:T(8,128)S(1)} %get-tuple-element.986), kind=kLoop, calls=%fused_computation.65.clone.1.clone | loop fusion | flops 39321600 | bytes 131092480 | tf_op jit(solution)/shard_map/while/body/eval_jaxpr/while/body/eval_jaxpr/convert_element_type | solution.py:278
  1160.7 22.1 fusion.238
  1182.8 44.9 %multiply_reduce_fusion.3 = (f32[8,640]{1,0:T(8,128)S(1)}, f32[8,640,2560]{2,1,0:T(8,128)}) fusion(f32[8,640,2560]{2,1,0:T(8,128)} %fusion.238, f32[8,640]{1,0:T(8,128)S(1)} %dynamic-slice_bitcast_fusion.3, bf16[4,1,2560,8,64]{2,4,3,1,0:T(8,128)(2,1)} %get-tuple-element.1049, s32[]{:T(128)} %get-tuple-element.1034, ...), kind=kOutput, calls=%fused_computation.66.clone.1.clone | convolution fusion | flops 1756359680 | bytes 109814784 | tf_op jit(solution)/shard_map/while/body/eval_jaxpr/while/body/eval_jaxpr/gqhe,gkhe->ghqk/dot_general | solution.py:193
  1227.7 42.2 %multiply_convert_fusion.4 = bf16[8,640,2560]{2,1,0:T(8,128)(2,1)} fusion(f32[8,640,2560]{2,1,0:T(8,128)} %get-tuple-element.985, f32[8,640,2560]{2,1,0:T(8,128)} %fusion.238, f32[8,640]{1,0:T(8,128)S(1)} %get-tuple-element.986), kind=kLoop, calls=%fused_computation.65.clone.1.clone | loop fusion | flops 39321600 | bytes 131092480 | tf_op jit(solution)/shard_map/while/body/eval_jaxpr/while/body/eval_jaxpr/convert_element_type | solution.py:278
  1322.5 21.7 fusion.238
  1344.2 44.8 %multiply_reduce_fusion.3 = (f32[8,640]{1,0:T(8,128)S(1)}, f32[8,640,2560]{2,1,0:T(8,128)}) fusion(f32[8,640,2560]{2,1,0:T(8,128)} %fusion.238, f32[8,640]{1,0:T(8,128)S(1)} %dynamic-slice_bitcast_fusion.3, bf16[4,1,2560,8,64]{2,4,3,1,0:T(8,128)(2,1)} %get-tuple-element.1049, s32[]{:T(128)} %get-tuple-element.1034, ...), kind=kOutput, calls=%fused_computation.66.clone.1.clone | convolution fusion | flops 1756359680 | bytes 109814784 | tf_op jit(solution)/shard_map/while/body/eval_jaxpr/while/body/eval_jaxpr/gqhe,gkhe->ghqk/dot_general | solution.py:193
  1389.0 41.6 %multiply_convert_fusion.4 = bf16[8,640,2560]{2,1,0:T(8,128)(2,1)} fusion(f32[8,640,2560]{2,1,0:T(8,128)} %get-tuple-element.985, f32[8,640,2560]{2,1,0:T(8,128)} %fusion.238, f32[8,640]{1,0:T(8,128)S(1)} %get-tuple-element.986), kind=kLoop, calls=%fused_computation.65.clone.1.clone | loop fusion | flops 39321600 | bytes 131092480 | tf_op jit(solution)/shard_map/while/body/eval_jaxpr/while/body/eval_jaxpr/convert_element_type | solution.py:278
  1482.6 21.7 fusion.238
  1504.3 44.7 %multiply_reduce_fusion.3 = (f32[8,640]{1,0:T(8,128)S(1)}, f32[8,640,2560]{2,1,0:T(8,128)}) fusion(f32[8,640,2560]{2,1,0:T(8,128)} %fusion.238, f32[8,640]{1,0:T(8,128)S(1)} %dynamic-slice_bitcast_fusion.3, bf16[4,1,2560,8,64]{2,4,3,1,0:T(8,128)(2,1)} %get-tuple-element.1049, s32[]{:T(128)} %get-tuple-element.1034, ...), kind=kOutput, calls=%fused_computation.66.clone.1.clone | convolution fusion | flops 1756359680 | bytes 109814784 | tf_op jit(solution)/shard_map/while/body/eval_jaxpr/while/body/eval_jaxpr/gqhe,gkhe->ghqk/dot_general | solution.py:193
  1549.0 41.6 %multiply_convert_fusion.4 = bf16[8,640,2560]{2,1,0:T(8,128)(2,1)} fusion(f32[8,640,2560]{2,1,0:T(8,128)} %get-tuple-element.985, f32[8,640,2560]{2,1,0:T(8,128)} %fusion.238, f32[8,640]{1,0:T(8,128)S(1)} %get-tuple-element.986), kind=kLoop, calls=%fused_computation.65.clone.1.clone | loop fusion | flops 39321600 | bytes 131092480 | tf_op jit(solution)/shard_map/while/body/eval_jaxpr/while/body/eval_jaxpr/convert_element_type | solution.py:278
  1639.9 42.3 %copy.60 = bf16[1,2560,2048]{2,0,1:T(2,128)(2,1)} copy(bf16[1,2560,2048]{1,2,0:T(8,128)(2,1)} %bitcast.366) | data formatting | bytes 20971520
  1698.5 42.9 %copy.62 = bf16[1,2560,2048]{2,0,1:T(2,128)(2,1)} copy(bf16[1,2560,2048]{1,2,0:T(8,128)(2,1)} %bitcast.367) | data formatting | bytes 20971520
  1762.3 34.5 %multiply_convert_fusion.1 = (bf16[640,8192]{1,0:T(8,128)(2,1)}, f32[640,8192]{1,0:T(8,128)}) fusion(f32[8192]{0:T(1024)S(1)} %convert_element_type.176, bf16[640,2048]{1,0:T(8,128)(2,1)} %fusion.104, bf16[2048,8192]{1,0:T(8,128)(2,1)} %all-gather.23.cloned.1.call-done), kind=kOutput, calls=%fused_computation.133 | convolution fusion | flops 21527265280 | bytes 67665920 | tf_op jit(solution)/shard_map/dot_general | solution.py:73
  1796.7 110.1 %while.70 = (s32[]{:T(128)}, bf16[4,2560,2048]{2,1,0:T(8,128)(2,1)}, s32[4]{0:T(128)S(1)}, bf16[640,2048]{0,1:T(8,128)(2,1)}, bf16[640,2048]{1,0:T(8,128)(2,1)S(...) while((s32[]{:T(128)}, bf16[4,2560,2048]{2,1,0:T(8,128)(2,1)}, s32[4]{0:T(128)S(1)}, ...), condition=%wide.region_24.25_spmd.clone, body=%wide.region_23.24_spmd.sunk.clone | while | flops 6731857920 | bytes 39977668 | solution.py:246
  1906.9 45.1 %convert_reduce_fusion = (f32[8192]{0:T(1024)}, bf16[640,8192]{1,0:T(8,128)(2,1)}) fusion(bf16[8192,2048]{1,0:T(8,128)(2,1)} %all-gather.27.cloned.1.call-done, bf16[1,640,2048]{2,1,0:T(8,128)(2,1)S(1)} %bitcast.373, f32[640,8192]{1,0:T(8,128)} %get-tuple-element.675, f32[8192]{0:T(1024)S(1)} %convert_element_type.176), kind=kOutput, calls=%fused_computation.132 | convolution fusion | flops 21616386048 | bytes 67698688 | tf_op jit(solution)/shard_map/dot_general | solution.py:83
  2017.2 148.8 %while.69 = (s32[]{:T(128)}, bf16[4,2048,3584]{1,2,0:T(8,128)(2,1)}, s32[4]{0:T(128)S(1)}, bf16[640,3,2048]{0,2,1:T(8,128)(2,1)}, bf16[640,2048]{1,0:T(8,128)(2,...) while((s32[]{:T(128)}, bf16[4,2048,3584]{1,2,0:T(8,128)(2,1)}, s32[4]{0:T(128)S(1)}, ...), condition=%wide.region_18.19_spmd.clone, body=%wide.region_17.18_spmd.sunk.clone | while | flops 9424601088 | bytes 93455112 | solution.py:351
  2166.0 40.5 %copy.67 = bf16[4,448,8,2048]{3,2,0,1:T(8,128)(2,1)} copy(bf16[4,448,8,2048]{3,2,1,0:T(8,128)(2,1)} %bitcast.347) | data formatting | bytes 117440512 | tf_op jit(solution)/shard_map/convert_element_type | solution.py:353
  2206.6 24.2 fusion.144
  2230.8 32.3 %fusion.137 = (f32[2048]{0:T(1024)}, f32[640]{0:T(1024)S(1)}, f32[640,2048]{1,0:T(8,128)}) fusion(f32[2048]{0:T(1024)S(1)} %copy-done.15, f32[640]{0:T(1024)S(1)} %copy-done.18, bf16[1,640,2048]{2,1,0:T(8,128)(2,1)S(1)} %copy-done.2, f32[640,2048]{1,0:T(8,128)} %fusion.144, bf16[640,8192]{1,0:T(8,128)(2,1)} %get-tuple-element.1235, ...), kind=kOutput, calls=%fused_computation.215 | convolution fusion | flops 21484009472 | bytes 57168896 | tf_op jit(solution)/shard_map/dot_general | solution.py:83
  2273.6 490.2 %reduce-scatter.13.cloned.1.call-done = bf16[2048,3584]{0,1:T(8,128)(2,1)} async-done(((bf16[8192,3584]{0,1:T(8,128)(2,1)}), bf16[2048,3584]{0,1:T(8,128)(2,1)}) %reduce-scatter.13.cloned.1.call-update) | async-done | bytes 14680080 | tf_op jit(solution)/shard_map/reduce_scatter | solution.py:352
  2764.5 26.8 fusion.143
  2800.9 92.6 %all-reduce.7.cloned.1.call-done = (f32[2048]{0:T(1024)}, f32[2048]{0:T(1024)}, f32[6144]{0:T(1024)}, f32[2048]{0:T(1024)}, f32[8192]{0:T(1024)}) async-done(((f32[2048]{0:T(1024)}, f32[2048]{0:T(1024)}, f32[6144]{0:T(1024)}, f32[2048]{0:T(1024)}, f32[8192]{0:T(1024)}), (f32[2048]{0:T(1024)}, f32[2048]{0:T(1024)}, f32[6144]{0:T(1024)}, f32[2048]{0:T(1024)}, f32[8192]{0:T(1024)})) %all-reduce.7.cloned.1.call-update) | async-done | bytes 81936 | tf_op jit(solution)/shard_map/psum | solution.py:378
  2893.5 113.0 %reduce-scatter.17.cloned.1.call-done = bf16[2560,256]{1,0:T(8,128)(2,1)} async-done(((bf16[2560,2048]{1,0:T(8,128)(2,1)}), bf16[2560,256]{1,0:T(8,128)(2,1)}) %reduce-scatter.17.cloned.1.call-update) | async-done | bytes 1310736 | tf_op jit(solution)/shard_map/reduce_scatter | solution.py:367
  3011.0 145.1 %reduce-scatter.15.cloned.1.call-done = bf16[256,3584]{0,1:T(8,128)(2,1)} async-done(((bf16[2048,3584]{0,1:T(8,128)(2,1)}), bf16[256,3584]{0,1:T(8,128)(2,1)}) %reduce-scatter.15.cloned.1.call-update) | async-done | bytes 1835024 | tf_op jit(solution)/shard_map/reduce_scatter | solution.py:368
  (357 shorter events, 678.4 us)
Async XLA Ops:
  7.2 78.6 %copy-start.33 = (bf16[2048]{0:T(1024)(128)(2,1)S(1)}, bf16[2048]{0:T(1024)(128)(2,1)}, u32[]{:S(2)}) copy-start(bf16[2048]{0:T(1024)(128)(2,1)} %param.24) | copy-start | bytes 12292
  7.2 78.6 %copy-start.34 = (bf16[2048]{0:T(1024)(128)(2,1)S(1)}, bf16[2048]{0:T(1024)(128)(2,1)}, u32[]{:S(2)}) copy-start(bf16[2048]{0:T(1024)(128)(2,1)} %param.25) | copy-start | bytes 12292
  7.2 78.6 %copy-start.30 = (bf16[6144]{0:T(1024)(128)(2,1)S(1)}, bf16[6144]{0:T(1024)(128)(2,1)}, u32[]{:S(2)}) copy-start(bf16[6144]{0:T(1024)(128)(2,1)} %param.27) | copy-start | bytes 36868
  7.2 78.6 %copy-start = (bf16[1,640,2048]{2,1,0:T(8,128)(2,1)S(1)}, bf16[1,640,2048]{2,1,0:T(8,128)(2,1)}, u32[]{:S(2)}) copy-start(bf16[1,640,2048]{2,1,0:T(8,128)(2,1)} %param.21) | copy-start | bytes 7864324
  7.2 50.0 %all-gather.13.cloned.1.call-start = ((), (), s32[]{:S(2)}) async-start(), calls=%async_computation.6 | async-start | bytes 3932160 | tf_op jit(solution)/shard_map/all_gather | solution.py:128
  9.7 76.0 %all-gather.17.cloned.1.call-start = ((), (), s32[]{:S(2)}) async-start(), calls=%async_computation.8 | async-start | bytes 1310720 | tf_op jit(solution)/shard_map/all_gather | solution.py:130
  10.5 298.0 %all-gather.15.cloned.1.call-start = ((), (), s32[]{:S(2)}) async-start(), calls=%async_computation.7 | async-start | bytes 28311552 | tf_op jit(solution)/shard_map/all_gather | solution.py:139
  57.2 309.8 %all-gather.21.cloned.1.call-start = ((), (), s32[]{:S(2)}) async-start(), calls=%async_computation.10 | async-start | bytes 5242880 | tf_op jit(solution)/shard_map/all_gather | solution.py:129
  57.8 358.0 %all-gather.25.cloned.1.call-start = ((), (), s32[]{:S(2)}) async-start(), calls=%async_computation.12 | async-start | bytes 5242880 | tf_op jit(solution)/shard_map/all_gather | solution.py:131
  58.4 441.4 %all-gather.19.cloned.1.call-start = ((), (), s32[]{:S(2)}) async-start(), calls=%async_computation.9 | async-start | bytes 9437184 | tf_op jit(solution)/shard_map/all_gather | solution.py:226
  85.7 519.8 %all-gather.29.cloned.1.call-start = ((), (), s32[]{:S(2)}) async-start(), calls=%async_computation.17 | async-start | bytes 13107200 | tf_op jit(solution)/shard_map/all_gather | solution.py:165
  85.8 245.3 %copy-start.13 = (f32[2048]{0:T(1024)}, f32[2048]{0:T(1024)S(1)}, u32[]{:S(2)}) copy-start(f32[2048]{0:T(1024)S(1)} %convert_element_type.166) | copy-start | bytes 24580
  85.8 245.3 %copy-start.24 = (f32[2048]{0:T(1024)}, f32[2048]{0:T(1024)S(1)}, u32[]{:S(2)}) copy-start(f32[2048]{0:T(1024)S(1)} %convert_element_type.167) | copy-start | bytes 24580
  86.3 244.8 %copy-start.16 = (f32[640]{0:T(1024)}, f32[640]{0:T(1024)S(1)}, u32[]{:S(2)}) copy-start(f32[640]{0:T(1024)S(1)} %broadcast_multiply_fusion) | copy-start | bytes 7684
  87.7 243.4 %copy-start.19 = (f32[640]{0:T(1024)}, f32[640]{0:T(1024)S(1)}, u32[]{:S(2)}) copy-start(f32[640]{0:T(1024)S(1)} %fusion.130) | copy-start | bytes 7684
  335.5 376.9 %all-gather.31.cloned.1.call-start = ((), (), s32[]{:S(2)}) async-start(), calls=%async_computation.18 | async-start | bytes 13107200 | tf_op jit(solution)/shard_map/all_gather | solution.py:164
  336.2 23.8 copy-start.9
  336.2 23.8 copy-start.11
  367.0 1395.3 %all-gather.23.cloned.1.call-start = ((), (), s32[]{:S(2)}) async-start(), calls=%async_computation.11 | async-start | bytes 37748736 | tf_op jit(solution)/shard_map/all_gather | solution.py:140
  367.7 1539.2 %all-gather.27.cloned.1.call-start = ((), (), s32[]{:S(2)}) async-start(), calls=%async_computation.13 | async-start | bytes 37748736 | tf_op jit(solution)/shard_map/all_gather | solution.py:227
  415.8 1536.2 %reduce-scatter.19.cloned.1.call-start = ((), (), s32[]{:S(2)}) async-start(), calls=%async_computation.19 | async-start | bytes 13107200
  1698.5 272.9 %reduce-scatter.21.cloned.1.call-start = ((), (), s32[]{:S(2)}) async-start(), calls=%async_computation.20 | async-start | bytes 13107200
  1758.0 515.1 %reduce-scatter.23.cloned.1.call-start = ((), (), s32[]{:S(2)}) async-start(), calls=%async_computation.21 | async-start | bytes 52428800
  1762.3 34.5 %copy-start.7 = (bf16[1,640,2048]{2,1,0:T(8,128)(2,1)S(1)}, bf16[1,640,2048]{2,1,0:T(8,128)(2,1)}, u32[]{:S(2)}) copy-start(bf16[1,640,2048]{2,1,0:T(8,128)(2,1)} %param.22) | copy-start | bytes 7864324
  1906.8 856.9 %reduce-scatter.13.cloned.1.call-start = ((), (), s32[]{:S(2)}) async-start(), calls=%async_computation.14 | async-start | bytes 73400320 | tf_op jit(solution)/shard_map/reduce_scatter | solution.py:352
  1978.0 17.3 slice-start.2
  1989.5 10.2 slice-start.4
  2001.8 7.8 copy-start.4
  2018.5 14.1 copy-start.5
  2030.4 7.5 slice-start
  2055.7 13.9 copy-start.5
  2067.7 7.2 slice-start
  2092.9 14.1 copy-start.5
  2105.0 7.3 slice-start
  2130.2 13.8 copy-start.5
  2142.1 7.2 slice-start
  2206.5 24.3 copy-start.2
  2206.5 24.3 copy-start.15
  2206.6 24.3 copy-start.18
  2206.6 687.0 %all-reduce.7.cloned.1.call-start = ((), (), s32[]{:S(2)}) async-start(), calls=%async_computation.22 | async-start | bytes 163840 | tf_op jit(solution)/shard_map/psum | solution.py:378
  2230.8 32.3 %copy-start.23 = (f32[640]{0:T(1024)S(1)}, f32[640]{0:T(1024)}, u32[]{:S(2)}) copy-start(f32[640]{0:T(1024)} %copy-done.22) | copy-start | bytes 7684
  2230.8 32.3 %copy-start.21 = (f32[640]{0:T(1024)S(1)}, f32[640]{0:T(1024)}, u32[]{:S(2)}) copy-start(f32[640]{0:T(1024)} %copy-done.19) | copy-start | bytes 7684
  2273.0 733.5 %reduce-scatter.17.cloned.1.call-start = ((), (), s32[]{:S(2)}) async-start(), calls=%async_computation.16 | async-start | bytes 11796480 | tf_op jit(solution)/shard_map/reduce_scatter | solution.py:367
  2273.6 882.5 %reduce-scatter.15.cloned.1.call-start = ((), (), s32[]{:S(2)}) async-start(), calls=%async_computation.15 | async-start | bytes 16515072 | tf_op jit(solution)/shard_map/reduce_scatter | solution.py:368
  2764.5 26.9 copy-start.6
  3157.4 5.9 copy-start.31
  3157.5 6.5 copy-start.28
  3157.5 7.7 copy-start.26
  (22 other events, 79.3 us)
Sparse Core Ops, SparseCore 0:
  10.5 46.6 all-gather.12
  59.0 26.6 all-gather.16
  87.3 221.1 all-gather.14
  310.2 51.2 all-gather.20
  363.1 52.6 all-gather.24
  417.2 82.4 all-gather.18
  502.2 103.2 all-gather.28
  607.3 105.0 all-gather.30
  714.0 288.6 all-gather.22
  1004.1 288.6 all-gather.26
  1698.6 104.0 reduce-scatter.18
  1805.6 103.5 reduce-scatter.20
  1912.3 356.3 reduce-scatter.22
  2271.9 491.8 reduce-scatter.12
  2771.2 122.2 all-reduce.6
  2895.7 110.7 reduce-scatter.16
  3008.6 147.3 reduce-scatter.14
where the time goes:
time: 3190 us; the launch traced here: 3170 us
  waiting for transfers between devices  1450 us (45%)
  matrix products  980 us (31%)
  other arithmetic  435 us (14%)
  local copies, waits for them, and re-layouts  276 us (9%)
    reduce_scatter x1, waiting for transfers between devices, shards(): lax.psum_scatter(blocks.reshape(span_rows, -1).astype(jnp.bfloat16), 'ctx...  490 us
    dot_general x8, matrix products, scores_of(): jnp.einsum('gqhe,gkhe->ghqk', query_part, key_part, preferred_element_typ...  274 us
    all_gather x1, waiting for transfers between devices, shards(): lax.all_gather(qkv_weight, 'fsdp', axis=0, tiled=True)  221 us
    convert_element_type x4, other arithmetic, backward_one_block(): score_grad = (weights * (weight_grad - inner)).astype(jnp.bfloat16)  168 us
    unnamed x99, local copies, waits for them, and re-layouts  165 us
    reduce_scatter x1, waiting for transfers between devices, shards(): lax.psum_scatter(in_local, 'fsdp', scatter_dimension=0, tiled=True)  145 us
    dot_general x16, matrix products, contract_rows(): lax.dot_general(left, right, (((0,), (0,)), ((), ())), preferred_element_...  122 us
    reduce_scatter x1, waiting for transfers between devices, shards(): lax.psum_scatter(out_local, 'fsdp', scatter_dimension=1, tiled=True)  113 us
  transfers between devices with their start and end apart: 17, of which 11 were waited for; matrix products, arithmetic and copies ran while one was open for 53% of the time, Pallas kernels for 0%

commit v1 on v0

--- a/solution.py
+++ b/solution.py
@@ -376,7 +376,8 @@
         (grad_values + token_grad_norm).astype(jnp.bfloat16).reshape(group_count, local_rows, width)
     )
     gain_sum, shift_sum, qkv_bias_sum, out_bias_sum, fc1_bias_sum = lax.psum(
-        (gain_grad, shift_grad, qkv_bias_grad, out_bias_grad, fc1_bias_part), ("ctx", "fsdp")
+        lax.psum((gain_grad, shift_grad, qkv_bias_grad, out_bias_grad, fc1_bias_part), "fsdp"),
+        "ctx",
     )
     return (
         output,

time: 3190 us -> 3310 us (1.038)
  waiting for transfers between devices: 1450 us -> 1580 us
    unnamed x20 -> x21, waiting for transfers between devices: 3.12 us -> 209 us
    psum x1, waiting for transfers between devices: 92.6 us -> 0.02 us  [shards(): lax.psum((gain_grad, shift_grad, qkv_bias_grad, out_bias_grad, fc1_bias_p...]
    unnamed x99 -> x97, local copies, waits for them, and re-layouts: 165 us -> 167 us
  transfers between devices with their start and end apart: 17 -> 18, of which waited for: 11 -> 13; matrix products, arithmetic and copies ran while one was open for 53% -> 48% of each run, Pallas kernels for 0% -> 0%
where the time goes in v1:
time: 3310 us; the launch traced here: 3290 us
  waiting for transfers between devices  1580 us (48%)
  matrix products  978 us (30%)
  other arithmetic  428 us (13%)
  local copies, waits for them, and re-layouts  278 us (8%)
    reduce_scatter x1, waiting for transfers between devices, shards(): lax.psum_scatter(blocks.reshape(span_rows, -1).astype(jnp.bfloat16), 'ctx...  495 us
    dot_general x8, matrix products, scores_of(): jnp.einsum('gqhe,gkhe->ghqk', query_part, key_part, preferred_element_typ...  274 us
    all_gather x1, waiting for transfers between devices, shards(): lax.all_gather(qkv_weight, 'fsdp', axis=0, tiled=True)  221 us
    unnamed x21, waiting for transfers between devices  209 us
    convert_element_type x4, other arithmetic, backward_one_block(): score_grad = (weights * (weight_grad - inner)).astype(jnp.bfloat16)  167 us
    unnamed x97, local copies, waits for them, and re-layouts  167 us
    reduce_scatter x1, waiting for transfers between devices, shards(): lax.psum_scatter(in_local, 'fsdp', scatter_dimension=0, tiled=True)  145 us
    dot_general x16, matrix products, contract_rows(): lax.dot_general(left, right, (((0,), (0,)), ((), ())), preferred_element_...  121 us
  transfers between devices with their start and end apart: 18, of which 13 were waited for; matrix products, arithmetic and copies ran while one was open for 48% of the time, Pallas kernels for 0%

profile of v1, /device:TPU:0, one launch (start us, length us, event | category | flops | bytes accessed | tf_op | source)
XLA Modules:
  0.0 3292.9 jit_solution(7837413047228973575)
XLA Ops:
  10.5 46.7 %all-gather.13.cloned.1.call-done = bf16[256,3,2048]{0,2,1:T(8,128)(2,1)} async-done(((bf16[256,3,512]{0,2,1:T(8,128)(2,1)}), bf16[256,3,2048]{0,2,1:T(8,128)(2,1)}) %all-gather.13.cloned.1.call-update) | async-done | bytes 3145744 | tf_op jit(solution)/shard_map/all_gather | solution.py:128
  58.4 27.3 all-gather.17.cloned.1.call-done
  87.7 220.7 %all-gather.15.cloned.1.call-done = bf16[2048,3,2048]{0,2,1:T(8,128)(2,1)} async-done(((bf16[256,3,2048]{0,2,1:T(8,128)(2,1)}), bf16[2048,3,2048]{0,2,1:T(8,128)(2,1)}) %all-gather.15.cloned.1.call-update) | async-done | bytes 25165840 | tf_op jit(solution)/shard_map/all_gather | solution.py:139
  308.5 22.6 convolution_add_fusion
  369.5 46.3 %all-gather.25.cloned.1.call-done = bf16[8192,256]{1,0:T(8,128)(2,1)} async-done(((bf16[2048,256]{1,0:T(8,128)(2,1)}), bf16[8192,256]{1,0:T(8,128)(2,1)}) %all-gather.25.cloned.1.call-update) | async-done | bytes 4194320 | tf_op jit(solution)/shard_map/all_gather | solution.py:131
  416.1 83.7 %all-gather.19.cloned.1.call-done = bf16[2048,2048]{1,0:T(8,128)(2,1)} async-done(((bf16[2048,256]{1,0:T(8,128)(2,1)}), bf16[2048,2048]{1,0:T(8,128)(2,1)}) %all-gather.19.cloned.1.call-update) | async-done | bytes 8388624 | tf_op jit(solution)/shard_map/all_gather | solution.py:226
  512.1 93.4 %all-gather.29.cloned.1.call-done = bf16[2560,2048]{1,0:T(8,128)(2,1)} async-done(((bf16[640,2048]{1,0:T(8,128)(2,1)}), bf16[2560,2048]{1,0:T(8,128)(2,1)}) %all-gather.29.cloned.1.call-update) | async-done | bytes 10485776 | tf_op jit(solution)/shard_map/all_gather | solution.py:165
  619.6 92.9 %all-gather.31.cloned.1.call-done = bf16[2560,2048]{0,1:T(8,128)(2,1)} async-done(((bf16[640,2048]{0,1:T(8,128)(2,1)}), bf16[2560,2048]{0,1:T(8,128)(2,1)}) %all-gather.31.cloned.1.call-update) | async-done | bytes 10485776 | tf_op jit(solution)/shard_map/all_gather | solution.py:164
  712.4 278.3 %while.71 = (s32[]{:T(128)}, bf16[4,1,640,8,64]{2,4,3,1,0:T(8,128)(2,1)}, f32[4,1,1,8,640,1]{4,3,5,2,1,0:T(8,128)S(1)}, bf16[4,1,2560,8,64]{2,4,3,1,0:T(8,128)(2...) while((s32[]{:T(128)}, ...), condition=%wide.region_5.6_spmd.clone.clone, body=%wide.region_2.5_spmd.clone.sunk.clone | while | flops 3520983552 | bytes 171326496 | solution.py:219
  715.5 27.3 fusion.228
  742.8 20.4 exponential_reduce_fusion.3
  763.2 22.7 fusion.229
  788.9 22.4 fusion.228
  811.4 20.4 exponential_reduce_fusion.3
  831.7 22.6 fusion.229
  857.4 22.4 fusion.228
  879.8 20.4 exponential_reduce_fusion.3
  900.2 22.6 fusion.229
  925.8 22.1 fusion.228
  968.3 22.5 fusion.229
  990.7 649.0 %while.72 = (s32[]{:T(128)}, f32[4,1,640,8,64]{2,4,3,1,0:T(8,128)}, bf16[4,1,2560,8,64]{2,4,3,1,0:T(8,128)(2,1)}, bf16[4,1,2560,8,64]{2,4,3,1,0:T(8,128)(2,1)}, ...) while((s32[]{:T(128)}, f32[4,1,640,8,64]{2,4,3,1,0:T(8,128)}, ...), condition=%wide.region_8.9_spmd.clone.clone, body=%wide.region_6.8_spmd.clone.sunk.clone | while | flops 8529572352 | bytes 418994240 | solution.py:308
  994.2 26.4 fusion.238
  1020.5 45.3 %multiply_reduce_fusion.3 = (f32[8,640]{1,0:T(8,128)S(1)}, f32[8,640,2560]{2,1,0:T(8,128)}) fusion(f32[8,640,2560]{2,1,0:T(8,128)} %fusion.238, f32[8,640]{1,0:T(8,128)S(1)} %dynamic-slice_bitcast_fusion.3, bf16[4,1,2560,8,64]{2,4,3,1,0:T(8,128)(2,1)} %get-tuple-element.1054, s32[]{:T(128)} %get-tuple-element.1039, ...), kind=kOutput, calls=%fused_computation.66.clone.1.clone | convolution fusion | flops 1756359680 | bytes 109814784 | tf_op jit(solution)/shard_map/while/body/eval_jaxpr/while/body/eval_jaxpr/gqhe,gkhe->ghqk/dot_general | solution.py:193
  1065.8 42.1 %multiply_convert_fusion.4 = bf16[8,640,2560]{2,1,0:T(8,128)(2,1)} fusion(f32[8,640,2560]{2,1,0:T(8,128)} %get-tuple-element.990, f32[8,640,2560]{2,1,0:T(8,128)} %fusion.238, f32[8,640]{1,0:T(8,128)S(1)} %get-tuple-element.991), kind=kLoop, calls=%fused_computation.65.clone.1.clone | loop fusion | flops 39321600 | bytes 131092480 | tf_op jit(solution)/shard_map/while/body/eval_jaxpr/while/body/eval_jaxpr/convert_element_type | solution.py:278
  1161.0 22.1 fusion.238
  1183.1 44.9 %multiply_reduce_fusion.3 = (f32[8,640]{1,0:T(8,128)S(1)}, f32[8,640,2560]{2,1,0:T(8,128)}) fusion(f32[8,640,2560]{2,1,0:T(8,128)} %fusion.238, f32[8,640]{1,0:T(8,128)S(1)} %dynamic-slice_bitcast_fusion.3, bf16[4,1,2560,8,64]{2,4,3,1,0:T(8,128)(2,1)} %get-tuple-element.1054, s32[]{:T(128)} %get-tuple-element.1039, ...), kind=kOutput, calls=%fused_computation.66.clone.1.clone | convolution fusion | flops 1756359680 | bytes 109814784 | tf_op jit(solution)/shard_map/while/body/eval_jaxpr/while/body/eval_jaxpr/gqhe,gkhe->ghqk/dot_general | solution.py:193
  1228.0 42.1 %multiply_convert_fusion.4 = bf16[8,640,2560]{2,1,0:T(8,128)(2,1)} fusion(f32[8,640,2560]{2,1,0:T(8,128)} %get-tuple-element.990, f32[8,640,2560]{2,1,0:T(8,128)} %fusion.238, f32[8,640]{1,0:T(8,128)S(1)} %get-tuple-element.991), kind=kLoop, calls=%fused_computation.65.clone.1.clone | loop fusion | flops 39321600 | bytes 131092480 | tf_op jit(solution)/shard_map/while/body/eval_jaxpr/while/body/eval_jaxpr/convert_element_type | solution.py:278
  1322.8 21.7 fusion.238
  1344.4 44.8 %multiply_reduce_fusion.3 = (f32[8,640]{1,0:T(8,128)S(1)}, f32[8,640,2560]{2,1,0:T(8,128)}) fusion(f32[8,640,2560]{2,1,0:T(8,128)} %fusion.238, f32[8,640]{1,0:T(8,128)S(1)} %dynamic-slice_bitcast_fusion.3, bf16[4,1,2560,8,64]{2,4,3,1,0:T(8,128)(2,1)} %get-tuple-element.1054, s32[]{:T(128)} %get-tuple-element.1039, ...), kind=kOutput, calls=%fused_computation.66.clone.1.clone | convolution fusion | flops 1756359680 | bytes 109814784 | tf_op jit(solution)/shard_map/while/body/eval_jaxpr/while/body/eval_jaxpr/gqhe,gkhe->ghqk/dot_general | solution.py:193
  1389.2 41.6 %multiply_convert_fusion.4 = bf16[8,640,2560]{2,1,0:T(8,128)(2,1)} fusion(f32[8,640,2560]{2,1,0:T(8,128)} %get-tuple-element.990, f32[8,640,2560]{2,1,0:T(8,128)} %fusion.238, f32[8,640]{1,0:T(8,128)S(1)} %get-tuple-element.991), kind=kLoop, calls=%fused_computation.65.clone.1.clone | loop fusion | flops 39321600 | bytes 131092480 | tf_op jit(solution)/shard_map/while/body/eval_jaxpr/while/body/eval_jaxpr/convert_element_type | solution.py:278
  1482.7 21.7 fusion.238
  1504.4 44.8 %multiply_reduce_fusion.3 = (f32[8,640]{1,0:T(8,128)S(1)}, f32[8,640,2560]{2,1,0:T(8,128)}) fusion(f32[8,640,2560]{2,1,0:T(8,128)} %fusion.238, f32[8,640]{1,0:T(8,128)S(1)} %dynamic-slice_bitcast_fusion.3, bf16[4,1,2560,8,64]{2,4,3,1,0:T(8,128)(2,1)} %get-tuple-element.1054, s32[]{:T(128)} %get-tuple-element.1039, ...), kind=kOutput, calls=%fused_computation.66.clone.1.clone | convolution fusion | flops 1756359680 | bytes 109814784 | tf_op jit(solution)/shard_map/while/body/eval_jaxpr/while/body/eval_jaxpr/gqhe,gkhe->ghqk/dot_general | solution.py:193
  1549.2 41.6 %multiply_convert_fusion.4 = bf16[8,640,2560]{2,1,0:T(8,128)(2,1)} fusion(f32[8,640,2560]{2,1,0:T(8,128)} %get-tuple-element.990, f32[8,640,2560]{2,1,0:T(8,128)} %fusion.238, f32[8,640]{1,0:T(8,128)S(1)} %get-tuple-element.991), kind=kLoop, calls=%fused_computation.65.clone.1.clone | loop fusion | flops 39321600 | bytes 131092480 | tf_op jit(solution)/shard_map/while/body/eval_jaxpr/while/body/eval_jaxpr/convert_element_type | solution.py:278
  1639.8 42.4 %copy.60 = bf16[1,2560,2048]{2,0,1:T(2,128)(2,1)} copy(bf16[1,2560,2048]{1,2,0:T(8,128)(2,1)} %bitcast.363) | data formatting | bytes 20971520
  1698.4 42.9 %copy.62 = bf16[1,2560,2048]{2,0,1:T(2,128)(2,1)} copy(bf16[1,2560,2048]{1,2,0:T(8,128)(2,1)} %bitcast.364) | data formatting | bytes 20971520
  1762.2 34.4 %multiply_convert_fusion.1 = (bf16[640,8192]{1,0:T(8,128)(2,1)}, f32[640,8192]{1,0:T(8,128)}) fusion(f32[8192]{0:T(1024)S(1)} %convert_element_type.176, bf16[640,2048]{1,0:T(8,128)(2,1)} %fusion.104, bf16[2048,8192]{1,0:T(8,128)(2,1)} %all-gather.23.cloned.1.call-done), kind=kOutput, calls=%fused_computation.133 | convolution fusion | flops 21527265280 | bytes 67665920 | tf_op jit(solution)/shard_map/dot_general | solution.py:73
  1796.6 45.2 %convert_reduce_fusion = (f32[8192]{0:T(1024)}, bf16[640,8192]{1,0:T(8,128)(2,1)}) fusion(bf16[8192,2048]{1,0:T(8,128)(2,1)} %all-gather.27.cloned.1.call-done, bf16[1,640,2048]{2,1,0:T(8,128)(2,1)S(1)} %copy-done.7, f32[640,8192]{1,0:T(8,128)} %get-tuple-element.680, f32[8192]{0:T(1024)S(1)} %convert_element_type.176), kind=kOutput, calls=%fused_computation.132 | convolution fusion | flops 21616386048 | bytes 67698688 | tf_op jit(solution)/shard_map/dot_general | solution.py:83
  1869.6 39.4 %reduce-scatter.21.cloned.1.call-done = bf16[640,2048]{1,0:T(8,128)(2,1)} async-done(((bf16[2560,2048]{1,0:T(8,128)(2,1)}), bf16[640,2048]{1,0:T(8,128)(2,1)}) %reduce-scatter.21.cloned.1.call-update) | async-done | bytes 2621456
  1940.3 23.4 fusion.144
  1963.7 31.7 fusion.137
  2005.4 111.2 %while.70 = (s32[]{:T(128)}, bf16[4,2560,2048]{2,1,0:T(8,128)(2,1)}, s32[4]{0:T(128)S(1)}, bf16[640,2048]{0,1:T(8,128)(2,1)}, bf16[640,2048]{1,0:T(8,128)(2,1)},...) while((s32[]{:T(128)}, bf16[4,2560,2048]{2,1,0:T(8,128)(2,1)}, s32[4]{0:T(128)S(1)}, ...), condition=%wide.region_27.28_spmd.clone, body=%wide.region_26.27_spmd.sunk.clone | while | flops 6731857920 | bytes 50463456 | solution.py:246
  2118.3 146.6 %while.69 = (s32[]{:T(128)}, bf16[4,2048,3584]{1,2,0:T(8,128)(2,1)}, s32[4]{0:T(128)S(1)}, bf16[640,3,2048]{0,2,1:T(8,128)(2,1)}, bf16[640,2048]{1,0:T(8,128)(2,...) while((s32[]{:T(128)}, bf16[4,2048,3584]{1,2,0:T(8,128)(2,1)}, ...), condition=%wide.region_20.21_spmd.clone, body=%wide.region_19.20_spmd.sunk.clone | while | flops 9424601088 | bytes 82969328 | solution.py:351
  2264.9 40.6 %copy.67 = bf16[4,448,8,2048]{3,2,0,1:T(8,128)(2,1)} copy(bf16[4,448,8,2048]{3,2,1,0:T(8,128)(2,1)} %bitcast.345) | data formatting | bytes 117440512 | tf_op jit(solution)/shard_map/convert_element_type | solution.py:353
  2306.2 166.9 %reduce-scatter.23.cloned.1.call-done = bf16[2560,2048]{1,0:T(8,128)(2,1)} async-done(((bf16[10240,2048]{1,0:T(8,128)(2,1)}), bf16[2560,2048]{1,0:T(8,128)(2,1)}) %reduce-scatter.23.cloned.1.call-update) | async-done | bytes 10485776
  2473.1 494.7 %reduce-scatter.13.cloned.1.call-done = bf16[2048,3584]{0,1:T(8,128)(2,1)} async-done(((bf16[8192,3584]{0,1:T(8,128)(2,1)}), bf16[2048,3584]{0,1:T(8,128)(2,1)}) %reduce-scatter.13.cloned.1.call-update) | async-done | bytes 14680080 | tf_op jit(solution)/shard_map/reduce_scatter | solution.py:352
  2968.6 26.9 fusion.143
  3013.9 112.6 %reduce-scatter.17.cloned.1.call-done = bf16[2560,256]{1,0:T(8,128)(2,1)} async-done(((bf16[2560,2048]{1,0:T(8,128)(2,1)}), bf16[2560,256]{1,0:T(8,128)(2,1)}) %reduce-scatter.17.cloned.1.call-update) | async-done | bytes 1310736 | tf_op jit(solution)/shard_map/reduce_scatter | solution.py:367
  3130.9 145.1 %reduce-scatter.15.cloned.1.call-done = bf16[256,3584]{0,1:T(8,128)(2,1)} async-done(((bf16[2048,3584]{0,1:T(8,128)(2,1)}), bf16[256,3584]{0,1:T(8,128)(2,1)}) %reduce-scatter.15.cloned.1.call-update) | async-done | bytes 1835024 | tf_op jit(solution)/shard_map/reduce_scatter | solution.py:368
  (357 shorter events, 701.5 us)
Async XLA Ops:
  7.2 78.6 %copy-start.34 = (bf16[2048]{0:T(1024)(128)(2,1)S(1)}, bf16[2048]{0:T(1024)(128)(2,1)}, u32[]{:S(2)}) copy-start(bf16[2048]{0:T(1024)(128)(2,1)} %param.24) | copy-start | bytes 12292
  7.2 78.6 %copy-start.35 = (bf16[2048]{0:T(1024)(128)(2,1)S(1)}, bf16[2048]{0:T(1024)(128)(2,1)}, u32[]{:S(2)}) copy-start(bf16[2048]{0:T(1024)(128)(2,1)} %param.25) | copy-start | bytes 12292
  7.2 78.6 %copy-start.31 = (bf16[6144]{0:T(1024)(128)(2,1)S(1)}, bf16[6144]{0:T(1024)(128)(2,1)}, u32[]{:S(2)}) copy-start(bf16[6144]{0:T(1024)(128)(2,1)} %param.27) | copy-start | bytes 36868
  7.2 78.6 %copy-start = (bf16[1,640,2048]{2,1,0:T(8,128)(2,1)S(1)}, bf16[1,640,2048]{2,1,0:T(8,128)(2,1)}, u32[]{:S(2)}) copy-start(bf16[1,640,2048]{2,1,0:T(8,128)(2,1)} %param.21) | copy-start | bytes 7864324
  7.2 50.0 %all-gather.13.cloned.1.call-start = ((), (), s32[]{:S(2)}) async-start(), calls=%async_computation.6 | async-start | bytes 3932160 | tf_op jit(solution)/shard_map/all_gather | solution.py:128
  9.7 76.0 %all-gather.17.cloned.1.call-start = ((), (), s32[]{:S(2)}) async-start(), calls=%async_computation.8 | async-start | bytes 1310720 | tf_op jit(solution)/shard_map/all_gather | solution.py:130
  10.5 298.0 %all-gather.15.cloned.1.call-start = ((), (), s32[]{:S(2)}) async-start(), calls=%async_computation.7 | async-start | bytes 28311552 | tf_op jit(solution)/shard_map/all_gather | solution.py:139
  57.2 309.7 %all-gather.21.cloned.1.call-start = ((), (), s32[]{:S(2)}) async-start(), calls=%async_computation.10 | async-start | bytes 5242880 | tf_op jit(solution)/shard_map/all_gather | solution.py:129
  57.8 358.0 %all-gather.25.cloned.1.call-start = ((), (), s32[]{:S(2)}) async-start(), calls=%async_computation.12 | async-start | bytes 5242880 | tf_op jit(solution)/shard_map/all_gather | solution.py:131
  58.4 441.4 %all-gather.19.cloned.1.call-start = ((), (), s32[]{:S(2)}) async-start(), calls=%async_computation.9 | async-start | bytes 9437184 | tf_op jit(solution)/shard_map/all_gather | solution.py:226
  85.7 519.8 %all-gather.29.cloned.1.call-start = ((), (), s32[]{:S(2)}) async-start(), calls=%async_computation.17 | async-start | bytes 13107200 | tf_op jit(solution)/shard_map/all_gather | solution.py:165
  85.8 245.3 %copy-start.14 = (f32[2048]{0:T(1024)}, f32[2048]{0:T(1024)S(1)}, u32[]{:S(2)}) copy-start(f32[2048]{0:T(1024)S(1)} %convert_element_type.166) | copy-start | bytes 24580
  85.8 245.3 %copy-start.25 = (f32[2048]{0:T(1024)}, f32[2048]{0:T(1024)S(1)}, u32[]{:S(2)}) copy-start(f32[2048]{0:T(1024)S(1)} %convert_element_type.167) | copy-start | bytes 24580
  86.3 244.8 %copy-start.17 = (f32[640]{0:T(1024)}, f32[640]{0:T(1024)S(1)}, u32[]{:S(2)}) copy-start(f32[640]{0:T(1024)S(1)} %broadcast_multiply_fusion) | copy-start | bytes 7684
  87.7 243.4 %copy-start.20 = (f32[640]{0:T(1024)}, f32[640]{0:T(1024)S(1)}, u32[]{:S(2)}) copy-start(f32[640]{0:T(1024)S(1)} %fusion.130) | copy-start | bytes 7684
  335.5 376.9 %all-gather.31.cloned.1.call-start = ((), (), s32[]{:S(2)}) async-start(), calls=%async_computation.18 | async-start | bytes 13107200 | tf_op jit(solution)/shard_map/all_gather | solution.py:164
  336.2 23.7 copy-start.10
  336.2 23.7 copy-start.12
  366.8 1395.3 %all-gather.23.cloned.1.call-start = ((), (), s32[]{:S(2)}) async-start(), calls=%async_computation.11 | async-start | bytes 37748736 | tf_op jit(solution)/shard_map/all_gather | solution.py:140
  367.6 1429.0 %all-gather.27.cloned.1.call-start = ((), (), s32[]{:S(2)}) async-start(), calls=%async_computation.13 | async-start | bytes 37748736 | tf_op jit(solution)/shard_map/all_gather | solution.py:227
  415.8 1425.9 %reduce-scatter.19.cloned.1.call-start = ((), (), s32[]{:S(2)}) async-start(), calls=%async_computation.19 | async-start | bytes 13107200
  1698.4 210.7 %reduce-scatter.21.cloned.1.call-start = ((), (), s32[]{:S(2)}) async-start(), calls=%async_computation.20 | async-start | bytes 13107200
  1757.9 547.8 %all-reduce.9.cloned.1.call-start = ((), (), s32[]{:S(2)}) async-start(), calls=%async_computation.22 | async-start | bytes 163840 | tf_op jit(solution)/shard_map/psum | solution.py:379
  1762.2 34.4 %copy-start.7 = (bf16[1,640,2048]{2,1,0:T(8,128)(2,1)S(1)}, bf16[1,640,2048]{2,1,0:T(8,128)(2,1)}, u32[]{:S(2)}) copy-start(bf16[1,640,2048]{2,1,0:T(8,128)(2,1)} %param.22) | copy-start | bytes 7864324
  1848.3 13.8 slice-start.2
  1940.3 23.4 copy-start.2
  1940.3 23.4 copy-start.16
  1940.3 23.4 copy-start.19
  1963.7 31.7 copy-start.24
  1963.7 31.7 copy-start.22
  2005.3 467.7 %reduce-scatter.23.cloned.1.call-start = ((), (), s32[]{:S(2)}) async-start(), calls=%async_computation.21 | async-start | bytes 52428800
  2006.7 11.9 copy-start.9
  2034.4 11.9 copy-start.9
  2062.2 11.9 copy-start.9
  2090.0 11.9 copy-start.9
  2116.6 851.3 %reduce-scatter.13.cloned.1.call-start = ((), (), s32[]{:S(2)}) async-start(), calls=%async_computation.14 | async-start | bytes 73400320 | tf_op jit(solution)/shard_map/reduce_scatter | solution.py:352
  2131.2 7.2 slice-start
  2167.6 7.2 slice-start
  2204.5 7.2 slice-start
  2241.1 7.2 slice-start
  2305.5 708.3 %all-reduce.11.cloned.1.call-start = ((), (), s32[]{:S(2)}) async-start(), calls=%async_computation.23 | async-start | bytes 163840 | tf_op jit(solution)/shard_map/psum | solution.py:378
  2306.1 820.3 %reduce-scatter.17.cloned.1.call-start = ((), (), s32[]{:S(2)}) async-start(), calls=%async_computation.16 | async-start | bytes 11796480 | tf_op jit(solution)/shard_map/reduce_scatter | solution.py:367
  2473.1 802.9 %reduce-scatter.15.cloned.1.call-start = ((), (), s32[]{:S(2)}) async-start(), calls=%async_computation.15 | async-start | bytes 16515072 | tf_op jit(solution)/shard_map/reduce_scatter | solution.py:368
  2968.6 27.0 copy-start.3
  2968.6 27.0 copy-start.6
  3277.4 5.9 copy-start.32
  3277.4 6.5 copy-start.29
  3277.4 7.7 copy-start.27
  (22 other events, 67.7 us)
Sparse Core Ops, SparseCore 0:
  10.5 46.6 all-gather.12
  59.0 26.6 all-gather.16
  87.3 221.1 all-gather.14
  310.2 51.2 all-gather.20
  363.1 52.6 all-gather.24
  417.2 82.4 all-gather.18
  502.2 103.2 all-gather.28
  607.3 105.0 all-gather.30
  714.0 288.6 all-gather.22
  1004.1 288.6 all-gather.26
  1698.5 103.9 reduce-scatter.18
  1805.5 103.5 reduce-scatter.20
  2005.5 50.6 all-reduce.8
  2116.7 356.3 reduce-scatter.22
  2476.0 491.8 reduce-scatter.12
  2971.6 42.2 all-reduce.10
  3016.0 110.3 reduce-scatter.16
  3128.6 147.3 reduce-scatter.14
